TPU v7x, 32 devices: a whole 2x2x4 slice. The times are simulated.
32 devices in a mesh: blk: 2 (over core), inner: 4 (over z), outer: 4 (over y, x).
Axes of the slice: x: 2, y: 2, z: 4, core: 2. Of those that a mesh axis runs over, the one named last changes fastest.
Arguments:
- hidden: bfloat16 [64, 256, 1152], P(('inner', 'outer'), 'blk'), may hold values from -6 to 6
- labels: int32 [64], P(('inner', 'outer')), may hold values from 0 to 1000
- steps_t: int32 [64], P(('inner', 'outer')), may hold values from 0 to 999
- live_slots: int32 [64], P(('inner', 'outer')), may hold values from 0 to 1, as said below
- label_table: bfloat16 [1001, 1152], replicated, may hold values from -6 to 6
- targets: bfloat16 [64, 256, 768], P(('inner', 'outer'), 'blk'), may hold values from -6 to 6
- cotangent: bfloat16 [64, 256, 1152], P(('inner', 'outer'), 'blk'), may hold values from -6 to 6
- weights: float32 [32014336], P(('inner', 'outer'))
- weight_momentum: float32 [32014336], P(('inner', 'outer')), may hold values from -320 to 320
- weight_average: float32 [32014336], P(('inner', 'outer'))
- biases: float32 [20992], P(('inner', 'outer')), may hold values from -1.25 to 1.25
- bias_momentum: float32 [20992], P(('inner', 'outer')), may hold values from -320 to 320
- bias_average: float32 [20992], P(('inner', 'outer')), may hold values from -1.25 to 1.25
Outputs:
- block_out: bfloat16 [64, 256, 1152], P(('inner', 'outer'), 'blk')
- grad_hidden: float32 [64, 256, 1152], P(('inner', 'outer'), 'blk')
- grad_cond: float32 [64, 1152], P(('inner', 'outer'))
- new_weight_momentum: float32 [32014336], P(('inner', 'outer'))
- new_weights: float32 [32014336], P(('inner', 'outer'))
- new_weights_low: bfloat16 [32014336], P(('inner', 'outer'))
- new_weight_average: float32 [32014336], P(('inner', 'outer'))
- new_bias_momentum: float32 [20992], P(('inner', 'outer'))
- new_biases: float32 [20992], P(('inner', 'outer'))
- new_biases_low: bfloat16 [20992], P(('inner', 'outer'))
- new_bias_average: float32 [20992], P(('inner', 'outer'))
Inputs may be any that keep to these rules, and one draw needn't show every extreme that they name: `live_slots`: of the 4 slots that one index of inner and outer holds at least one is live, and in the last such index all are.
All inputs are finite; a program needn't handle non-finite values.
Results may differ from a plain program's by a relative error of at most 0.02.
The roundings to bfloat16 on the way count: a program that leaves them out, or rounds other values in their place, can miss the bound.
Values may be sent and summed in bfloat16 or wider, within the bound.
No kernel may reach another device: no remote copies, remote signals or barrier semaphores. Data moves between devices by JAX's collectives and lax.ppermute only.
A program may use at most 384 MiB of HBM per device.

v0:
```python
import math
import jax
import jax.numpy as jnp
from jax import lax
from jax.sharding import PartitionSpec as P

E = 72
D = 1152
FF = 4608
PH = 2048
ZD = 768
LAMBDA_REPA = 0.5
MOMENTUM = 0.5
AVERAGE = 0.5
LR_COEF = 0.04
BIAS_FACTOR = 4.0
EPS_NORM = 1e-06


def passed_along(block, axis, distance):
    devices = range(lax.axis_size(axis))
    route = [((i - distance) % len(devices), i) for i in devices]
    return lax.ppermute(block, axis, route)


def mat_shapes():
    return [(D, 3 * D), (D, D), (D, FF), (FF, D), (D, 6 * D), (D, PH), (PH, PH), (PH, ZD)]


def bias_shapes():
    return [(D,), (D,), (D,), (FF,), (D,), (6 * D,), (PH,), (PH,), (ZD,)]


def split_shard(flat_vec, shapes, blocks):
    segments = []
    offset = 0
    for shape_now in shapes:
        rows_here = shape_now[0] // blocks
        length = rows_here * math.prod(shape_now[1:])
        segments.append(
            flat_vec[offset : offset + length].reshape((rows_here,) + tuple(shape_now[1:]))
        )
        offset += length
    return segments


def unpack_rows(flat_vec, shapes, blocks):
    line_grid = flat_vec.reshape(blocks, -1)
    segments = []
    offset = 0
    for shape_now in shapes:
        length = shape_now[0] // blocks * math.prod(shape_now[1:])
        segments.append(line_grid[:, offset : offset + length].reshape(shape_now))
        offset += length
    return segments


def outer_grid(segments, n_outer):
    grid_w = jnp.concatenate([segment.reshape(n_outer, -1) for segment in segments[:8]], axis=1)
    return (grid_w, segments[8].reshape(n_outer, -1))


def time_embed(steps_t):
    half_dim = D // 2
    frequency = jnp.exp(-math.log(10000.0) * jnp.arange(half_dim, dtype=jnp.float32) / half_dim)
    angles = steps_t.astype(jnp.float32)[:, None] * frequency[None, :]
    return jnp.concatenate([jnp.cos(angles), jnp.sin(angles)], axis=1)


def modulate(values, scale_v, shift_v):
    center = values - jnp.mean(values, axis=-1, keepdims=True)
    normed = center * lax.rsqrt(jnp.mean(center * center, axis=-1, keepdims=True) + EPS_NORM)
    return normed * (1.0 + scale_v[:, None, :]) + shift_v[:, None, :]


def gelu_tanh(values):
    return jax.nn.gelu(values, approximate=True)


def rms_unit(values):
    return values * lax.rsqrt(jnp.mean(values * values, axis=-1, keepdims=True) + EPS_NORM)


def matmul(left_arr, right_arr):
    return jnp.einsum("...i,ij->...j", left_arr, right_arr, preferred_element_type=jnp.float32)


def matmul_t(left_arr, right_arr):
    return jnp.einsum("...j,ij->...i", left_arr, right_arr, preferred_element_type=jnp.float32)


def outer_sum(left_arr, right_arr):
    return jnp.einsum("sni,snj->ij", left_arr, right_arr, preferred_element_type=jnp.float32)


def column_sum(tensor):
    return jnp.sum(tensor.astype(jnp.float32), axis=(0, 1))


def head_view(tensor):
    return tensor.reshape(tensor.shape[0], tensor.shape[1], -1, E)


def score_block(queries, kv_pair):
    raw_scores = jnp.einsum(
        "snhe,smhe->shnm",
        head_view(queries),
        head_view(kv_pair[..., :D]),
        preferred_element_type=jnp.float32,
    )
    return raw_scores * E ** (-0.5)


def weigh_values(probs_blk, kv_pair):
    mixed_out = jnp.einsum(
        "shnm,smhe->snhe",
        probs_blk.astype(jnp.bfloat16),
        head_view(kv_pair[..., D:]),
        preferred_element_type=jnp.float32,
    )
    return mixed_out.reshape(mixed_out.shape[0], mixed_out.shape[1], D)


def grad_block(queries, kv_pair, log_sum, grad_att):
    probs_blk = jnp.exp(score_block(queries, kv_pair) - log_sum[..., None])
    grad_prob = jnp.einsum(
        "snhe,smhe->shnm",
        head_view(grad_att),
        head_view(kv_pair[..., D:]),
        preferred_element_type=jnp.float32,
    )
    return (probs_blk, grad_prob)


def key_product(grad_scores, kv_pair):
    result = jnp.einsum(
        "shnm,smhe->snhe",
        grad_scores,
        head_view(kv_pair[..., :D]),
        preferred_element_type=jnp.float32,
    )
    return result.reshape(result.shape[0], result.shape[1], D)


def kv_grads(grad_scores, probs_blk, queries, grad_att):
    grad_keys = jnp.einsum(
        "shnm,snhe->smhe", grad_scores, head_view(queries), preferred_element_type=jnp.float32
    ) * E ** (-0.5)
    grad_vals = jnp.einsum(
        "shnm,snhe->smhe",
        probs_blk.astype(jnp.bfloat16),
        head_view(grad_att),
        preferred_element_type=jnp.float32,
    )
    rows_n = grad_keys.shape[1]
    return jnp.concatenate(
        [
            grad_keys.reshape(grad_keys.shape[0], rows_n, D),
            grad_vals.reshape(grad_vals.shape[0], rows_n, D),
        ],
        axis=-1,
    )


def body(
    hidden,
    labels,
    steps_t,
    live_slots,
    label_table,
    targets,
    cotangent,
    weights,
    weight_momentum,
    weight_average,
    biases,
    bias_momentum,
    bias_average,
):
    n_inner = lax.axis_size("inner")
    n_outer = lax.axis_size("outer")
    blocks = n_inner * n_outer
    slots = hidden.shape[0]
    local_tok = hidden.shape[1]
    p_qkv, p_proj, p_up, p_down, p_ada, p_one, p_two, p_three = split_shard(
        weights.astype(jnp.bfloat16), mat_shapes(), blocks
    )
    bias_low = biases.astype(jnp.bfloat16)
    w_qkv, w_proj, w_up, w_down, w_ada, w_one, w_two, w_three, bias_all = (
        lax.all_gather(p_qkv, ("inner", "outer"), axis=0, tiled=True),
        lax.all_gather(p_proj, ("inner", "outer"), axis=0, tiled=True),
        lax.all_gather(p_up, ("inner", "outer"), axis=0, tiled=True),
        lax.all_gather(p_down, ("inner", "outer"), axis=0, tiled=True),
        lax.all_gather(p_ada, ("inner", "outer"), axis=0, tiled=True),
        lax.all_gather(p_one, ("inner", "outer"), axis=0, tiled=True),
        lax.all_gather(p_two, ("inner", "outer"), axis=0, tiled=True),
        lax.all_gather(p_three, ("inner", "outer"), axis=0, tiled=True),
        lax.all_gather(bias_low, ("inner", "outer"), axis=0, tiled=True),
    )
    b_q, b_v, b_proj, b_up, b_down, b_ada, c_one, c_two, c_three = unpack_rows(
        bias_all.astype(jnp.float32), bias_shapes(), blocks
    )
    condition = label_table[labels].astype(jnp.float32) + time_embed(steps_t)
    cond_act, silu_cond = jax.vjp(jax.nn.silu, condition)
    cond_low = cond_act.astype(jnp.bfloat16)
    modulation = matmul(cond_low, w_ada) + b_ada
    shift_a, scale_a, gate_a, shift_m, scale_m, gate_m = [
        modulation[:, part_idx * D : (part_idx + 1) * D] for part_idx in range(6)
    ]
    hidden_f = hidden.astype(jnp.float32)
    mixed_a, pull_a = jax.vjp(modulate, hidden_f, scale_a, shift_a)
    mixed_a_low = mixed_a.astype(jnp.bfloat16)
    qkv_bias = jnp.concatenate([b_q, jnp.zeros((D,), jnp.float32), b_v])
    qkv_low = (matmul(mixed_a_low, w_qkv) + qkv_bias).astype(jnp.bfloat16)
    queries = qkv_low[..., :D]
    near_kv = qkv_low[..., D:]
    far_kv = passed_along(near_kv, "blk", 1)
    near_s = score_block(queries, near_kv)
    far_s = score_block(queries, far_kv)
    row_top = jnp.maximum(jnp.max(near_s, axis=-1), jnp.max(far_s, axis=-1))
    row_total = jnp.sum(jnp.exp(near_s - row_top[..., None]), axis=-1) + jnp.sum(
        jnp.exp(far_s - row_top[..., None]), axis=-1
    )
    log_sum = row_top + jnp.log(row_total)
    attended = weigh_values(jnp.exp(near_s - log_sum[..., None]), near_kv) + weigh_values(
        jnp.exp(far_s - log_sum[..., None]), far_kv
    )
    att_low = attended.astype(jnp.bfloat16)
    branch_a = matmul(att_low, w_proj) + b_proj
    residual = hidden_f + gate_a[:, None, :] * branch_a
    mixed_m, pull_m = jax.vjp(modulate, residual, scale_m, shift_m)
    mixed_m_low = mixed_m.astype(jnp.bfloat16)
    pre_act = matmul(mixed_m_low, w_up) + b_up
    activated, gelu_pull = jax.vjp(gelu_tanh, pre_act)
    act_low = activated.astype(jnp.bfloat16)
    branch_m = matmul(act_low, w_down) + b_down
    output = residual + gate_m[:, None, :] * branch_m
    out_low = output.astype(jnp.bfloat16)
    hid_one = matmul(out_low, w_one) + c_one
    act_one, silu_one = jax.vjp(jax.nn.silu, hid_one)
    one_low = act_one.astype(jnp.bfloat16)
    hid_two = matmul(one_low, w_two) + c_two
    act_two, silu_two = jax.vjp(jax.nn.silu, hid_two)
    two_low = act_two.astype(jnp.bfloat16)
    projection = matmul(two_low, w_three) + c_three
    live_f = live_slots.astype(jnp.float32)[:, None, None]
    unit_proj, unit_pull = jax.vjp(rms_unit, projection)
    grad_proj = unit_pull(-LAMBDA_REPA * live_f * rms_unit(targets.astype(jnp.float32)))[0].astype(
        jnp.bfloat16
    )
    grad_pthree = outer_sum(two_low, grad_proj)
    grad_cthree = column_sum(grad_proj)
    grad_htwo = silu_two(matmul_t(grad_proj, w_three))[0].astype(jnp.bfloat16)
    grad_ptwo = outer_sum(one_low, grad_htwo)
    grad_ctwo = column_sum(grad_htwo)
    grad_hone = silu_one(matmul_t(grad_htwo, w_two))[0].astype(jnp.bfloat16)
    grad_pone = outer_sum(out_low, grad_hone)
    grad_cone = column_sum(grad_hone)
    grad_output = cotangent.astype(jnp.float32) * live_f + matmul_t(grad_hone, w_one)
    grad_gate_m = jnp.sum(grad_output * branch_m, axis=1)
    grad_bm = (gate_m[:, None, :] * grad_output).astype(jnp.bfloat16)
    grad_wdown = outer_sum(act_low, grad_bm)
    grad_bdown = column_sum(grad_bm)
    grad_pre = gelu_pull(matmul_t(grad_bm, w_down))[0].astype(jnp.bfloat16)
    grad_wup = outer_sum(mixed_m_low, grad_pre)
    grad_bup = column_sum(grad_pre)
    grad_res_m, grad_scale_m, grad_shift_m = pull_m(matmul_t(grad_pre, w_up))
    grad_residual = grad_output + grad_res_m
    grad_gate_a = jnp.sum(grad_residual * branch_a, axis=1)
    grad_ba = (gate_a[:, None, :] * grad_residual).astype(jnp.bfloat16)
    grad_wproj = outer_sum(att_low, grad_ba)
    grad_bproj = column_sum(grad_ba)
    grad_att = matmul_t(grad_ba, w_proj).astype(jnp.bfloat16)
    near_p, near_dp = grad_block(queries, near_kv, log_sum, grad_att)
    far_p, far_dp = grad_block(queries, far_kv, log_sum, grad_att)
    row_delta = jnp.sum(near_p * near_dp, axis=-1) + jnp.sum(far_p * far_dp, axis=-1)
    near_ds = (near_p * (near_dp - row_delta[..., None])).astype(jnp.bfloat16)
    far_ds = (far_p * (far_dp - row_delta[..., None])).astype(jnp.bfloat16)
    grad_query = (key_product(near_ds, near_kv) + key_product(far_ds, far_kv)) * E ** (-0.5)
    far_dkv = kv_grads(far_ds, far_p, queries, grad_att)
    home_dkv = passed_along(far_dkv.astype(jnp.bfloat16), "blk", -1).astype(far_dkv.dtype)
    near_dkv = kv_grads(near_ds, near_p, queries, grad_att)
    grad_qkv = jnp.concatenate([grad_query, near_dkv + home_dkv], axis=-1).astype(jnp.bfloat16)
    grad_wqkv = outer_sum(mixed_a_low, grad_qkv)
    qkv_sums = column_sum(grad_qkv)
    grad_hid_a, grad_scale_a, grad_shift_a = pull_a(matmul_t(grad_qkv, w_qkv))
    grad_input = grad_residual + grad_hid_a
    grad_mod_part = jnp.concatenate(
        [grad_shift_a, grad_scale_a, grad_gate_a, grad_shift_m, grad_scale_m, grad_gate_m], axis=1
    )
    grad_mod = lax.psum(grad_mod_part.astype(jnp.bfloat16), "blk")
    grad_wada = 0.5 * jnp.einsum(
        "si,sj->ij", cond_low, grad_mod, preferred_element_type=jnp.float32
    )
    grad_bada = 0.5 * jnp.sum(grad_mod.astype(jnp.float32), axis=0)
    grad_cond = silu_cond(matmul_t(grad_mod, w_ada))[0]
    bias_terms = (
        qkv_sums[:D],
        qkv_sums[2 * D :],
        grad_bproj,
        grad_bup,
        grad_bdown,
        grad_bada,
        grad_cone,
        grad_ctwo,
        grad_cthree,
    )
    bias_grid = jnp.concatenate(
        [segment.reshape(blocks, -1) for segment in bias_terms], axis=1
    ).reshape(-1)
    inner_parts = (
        lax.psum_scatter(
            grad_wqkv.astype(jnp.bfloat16), "inner", scatter_dimension=0, tiled=True
        ).astype(jnp.float32),
        lax.psum_scatter(
            grad_wproj.astype(jnp.bfloat16), "inner", scatter_dimension=0, tiled=True
        ).astype(jnp.float32),
        lax.psum_scatter(
            grad_wup.astype(jnp.bfloat16), "inner", scatter_dimension=0, tiled=True
        ).astype(jnp.float32),
        lax.psum_scatter(
            grad_wdown.astype(jnp.bfloat16), "inner", scatter_dimension=0, tiled=True
        ).astype(jnp.float32),
        lax.psum_scatter(
            grad_wada.astype(jnp.bfloat16), "inner", scatter_dimension=0, tiled=True
        ).astype(jnp.float32),
        lax.psum_scatter(
            grad_pone.astype(jnp.bfloat16), "inner", scatter_dimension=0, tiled=True
        ).astype(jnp.float32),
        lax.psum_scatter(
            grad_ptwo.astype(jnp.bfloat16), "inner", scatter_dimension=0, tiled=True
        ).astype(jnp.float32),
        lax.psum_scatter(
            grad_pthree.astype(jnp.bfloat16), "inner", scatter_dimension=0, tiled=True
        ).astype(jnp.float32),
        lax.psum_scatter(
            bias_grid.astype(jnp.bfloat16), "inner", scatter_dimension=0, tiled=True
        ).astype(jnp.float32),
    )
    grid_w, grid_b = outer_grid(inner_parts, n_outer)
    summed_w, summed_b = (
        lax.psum(grid_w.astype(jnp.bfloat16), ("blk", "outer")).astype(jnp.float32),
        lax.psum(grid_b.astype(jnp.bfloat16), ("blk", "outer")).astype(jnp.float32),
    )
    own_index = lax.axis_index("outer")
    grad_w_flat = lax.dynamic_index_in_dim(summed_w, own_index, 0, keepdims=False)
    grad_b_flat = lax.dynamic_index_in_dim(summed_b, own_index, 0, keepdims=False)
    images_all = slots * blocks
    tokens_img = local_tok * lax.axis_size("blk")
    rate_w = LR_COEF / math.sqrt(images_all * tokens_img)
    rate_b = BIAS_FACTOR * rate_w
    mom_w = MOMENTUM * weight_momentum + grad_w_flat
    new_w = weights - rate_w * (grad_w_flat + MOMENTUM * mom_w)
    avg_w = AVERAGE * weight_average + (1.0 - AVERAGE) * new_w
    mom_b = MOMENTUM * bias_momentum + grad_b_flat
    new_b = biases - rate_b * (grad_b_flat + MOMENTUM * mom_b)
    avg_b = AVERAGE * bias_average + (1.0 - AVERAGE) * new_b
    return (
        out_low,
        grad_input,
        grad_cond,
        mom_w,
        new_w,
        new_w.astype(jnp.bfloat16),
        avg_w,
        mom_b,
        new_b,
        new_b.astype(jnp.bfloat16),
        avg_b,
    )


def solution(mesh):
    in_specs = (
        P(("inner", "outer"), "blk", None),
        P(("inner", "outer")),
        P(("inner", "outer")),
        P(("inner", "outer")),
        P(),
        P(("inner", "outer"), "blk", None),
        P(("inner", "outer"), "blk", None),
        P(("inner", "outer")),
        P(("inner", "outer")),
        P(("inner", "outer")),
        P(("inner", "outer")),
        P(("inner", "outer")),
        P(("inner", "outer")),
    )
    out_specs = (
        P(("inner", "outer"), "blk", None),
        P(("inner", "outer"), "blk", None),
        P(("inner", "outer"), None),
        P(("inner", "outer")),
        P(("inner", "outer")),
        P(("inner", "outer")),
        P(("inner", "outer")),
        P(("inner", "outer")),
        P(("inner", "outer")),
        P(("inner", "outer")),
        P(("inner", "outer")),
    )
    return jax.shard_map(body, mesh=mesh, in_specs=in_specs, out_specs=out_specs, check_vma=False)
```

profile of v0, /device:TPU:0, one launch (start us, length us, event | category | flops | bytes accessed | tf_op | source)
XLA Modules:
  0.0 2376.6 jit_solution(2534763386764745877)
XLA Ops:
  35.4 80.9 %all-reduce = bf16[20992]{0:T(1024)(128)(2,1)} all-reduce(bf16[20992]{0:T(1024)(128)(2,1)S(1)} %dynamic-update-slice), channel_id=1, replica_groups=mesh['blk'=2,'inner'=4,'outer'=4] {'inner','outer'}, use_global_device_ids=true, to_apply=%add | all-reduce | flops 20992 | bytes 83968
  125.7 79.5 %all-gather.9.cloned.1.call-done = bf16[1152,6912]{1,0:T(8,128)(2,1)} async-done(((bf16[72,6912]{1,0:T(8,128)(2,1)}), bf16[1152,6912]{1,0:T(8,128)(2,1)}) %all-gather.9.cloned.1.call-update) | async-done | bytes 15925264 | tf_op jit(solution)/shard_map/all_gather | solution.py:194
  213.0 102.7 %all-gather.11.cloned.1.call-done = bf16[1152,3456]{1,0:T(8,128)(2,1)} async-done(((bf16[72,3456]{1,0:T(8,128)(2,1)}), bf16[1152,3456]{1,0:T(8,128)(2,1)}) %all-gather.11.cloned.1.call-update) | async-done | bytes 7962640 | tf_op jit(solution)/shard_map/all_gather | solution.py:190
  365.8 15.1 all-gather.13.cloned.1.call-done
  388.3 127.6 %all-gather.15.cloned.1.call-done = bf16[1152,4608]{1,0:T(8,128)(2,1)} async-done(((bf16[72,4608]{1,0:T(8,128)(2,1)}), bf16[1152,4608]{1,0:T(8,128)(2,1)}) %all-gather.15.cloned.1.call-update) | async-done | bytes 10616848 | tf_op jit(solution)/shard_map/all_gather | solution.py:192
  516.0 12.2 fusion.9
  528.1 122.7 %all-gather.17.cloned.1.call-done = bf16[4608,1152]{1,0:T(8,128)(2,1)} async-done(((bf16[288,1152]{1,0:T(8,128)(2,1)}), bf16[4608,1152]{1,0:T(8,128)(2,1)}) %all-gather.17.cloned.1.call-update) | async-done | bytes 10616848 | tf_op jit(solution)/shard_map/all_gather | solution.py:193
  650.9 14.5 add_convert_fusion.1
  665.4 66.8 %all-gather.19.cloned.1.call-done = bf16[1152,2048]{1,0:T(8,128)(2,1)} async-done(((bf16[72,2048]{1,0:T(8,128)(2,1)}), bf16[1152,2048]{1,0:T(8,128)(2,1)}) %all-gather.19.cloned.1.call-update) | async-done | bytes 4718608 | tf_op jit(solution)/shard_map/all_gather | solution.py:195
  738.9 107.6 %all-gather.21.cloned.1.call-done = bf16[2048,2048]{1,0:T(8,128)(2,1)} async-done(((bf16[128,2048]{1,0:T(8,128)(2,1)}), bf16[2048,2048]{1,0:T(8,128)(2,1)}) %all-gather.21.cloned.1.call-update) | async-done | bytes 8388624 | tf_op jit(solution)/shard_map/all_gather | solution.py:196
  857.7 57.9 %all-gather.23.cloned.1.call-done = bf16[2048,768]{1,0:T(8,128)(2,1)} async-done(((bf16[128,768]{1,0:T(8,128)(2,1)}), bf16[2048,768]{1,0:T(8,128)(2,1)}) %all-gather.23.cloned.1.call-update) | async-done | bytes 3145744 | tf_op jit(solution)/shard_map/all_gather | solution.py:197
  941.9 17.3 fusion.114
  959.2 12.2 multiply_reduce_fusion.7
  1085.1 13.1 fusion.1
  1132.1 48.8 %reduce-scatter.19.cloned.1.call-done = bf16[288,2048]{1,0:T(8,128)(2,1)} async-done(((bf16[1152,2048]{1,0:T(8,128)(2,1)}), bf16[288,2048]{1,0:T(8,128)(2,1)}) %reduce-scatter.19.cloned.1.call-update) | async-done | bytes 1179664 | tf_op jit(solution)/shard_map/reduce_scatter | solution.py:327
  1184.1 144.1 %reduce-scatter.21.cloned.1.call-done = bf16[512,2048]{1,0:T(8,128)(2,1)} async-done(((bf16[2048,2048]{1,0:T(8,128)(2,1)}), bf16[512,2048]{1,0:T(8,128)(2,1)}) %reduce-scatter.21.cloned.1.call-update) | async-done | bytes 2097168 | tf_op jit(solution)/shard_map/reduce_scatter | solution.py:330
  1331.4 138.6 %reduce-scatter.9.cloned.1.call-done = bf16[288,3456]{1,0:T(8,128)(2,1)} async-done(((bf16[1152,3456]{1,0:T(8,128)(2,1)}), bf16[288,3456]{1,0:T(8,128)(2,1)}) %reduce-scatter.9.cloned.1.call-update) | async-done | bytes 1990672 | tf_op jit(solution)/shard_map/reduce_scatter | solution.py:312
  1477.9 175.2 %reduce-scatter.13.cloned.1.call-done = bf16[288,4608]{1,0:T(8,128)(2,1)} async-done(((bf16[1152,4608]{1,0:T(8,128)(2,1)}), bf16[288,4608]{1,0:T(8,128)(2,1)}) %reduce-scatter.13.cloned.1.call-update) | async-done | bytes 2654224 | tf_op jit(solution)/shard_map/reduce_scatter | solution.py:318
  1662.9 173.6 %reduce-scatter.15.cloned.1.call-done = bf16[1152,1152]{1,0:T(8,128)(2,1)} async-done(((bf16[4608,1152]{1,0:T(8,128)(2,1)}), bf16[1152,1152]{1,0:T(8,128)(2,1)}) %reduce-scatter.15.cloned.1.call-update) | async-done | bytes 2654224 | tf_op jit(solution)/shard_map/reduce_scatter | solution.py:321
  1845.2 262.1 %reduce-scatter.17.cloned.1.call-done = bf16[288,6912]{1,0:T(8,128)(2,1)} async-done(((bf16[1152,6912]{1,0:T(8,128)(2,1)}), bf16[288,6912]{1,0:T(8,128)(2,1)}) %reduce-scatter.17.cloned.1.call-update) | async-done | bytes 3981328 | tf_op jit(solution)/shard_map/reduce_scatter | solution.py:324
  2129.0 18.7 all-reduce.1
  2148.0 29.0 %psum.23 = bf16[4,1312]{1,0:T(4,128)(2,1)S(1)} all-reduce(bf16[4,1312]{1,0:T(4,128)(2,1)S(1)} %convert_element_type.227), channel_id=1, replica_groups=mesh['blk'=2,'inner'=4,'outer'=4] {'blk','outer'}, use_global_device_ids=true, to_apply=%region_42.43 | all-reduce | flops 5248 | bytes 20992 | tf_op jit(solution)/shard_map/psum | solution.py:343
  2188.9 146.4 %all-reduce.4.cloned.1.call-done = bf16[4,2000896]{1,0:T(4,128)(2,1)} async-done(((bf16[4,2000896]{1,0:T(4,128)(2,1)}), bf16[4,2000896]{1,0:T(4,128)(2,1)}) %all-reduce.4.cloned.1.call-update) | async-done | bytes 16007184 | tf_op jit(solution)/shard_map/psum | solution.py:342
  2344.8 20.1 add_multiply_fusion
  (379 shorter events, 373.5 us)
Async XLA Ops:
  7.2 116.3 %copy-start = (bf16[1001,1152]{1,0:T(8,128)(2,1)S(1)}, bf16[1001,1152]{1,0:T(8,128)(2,1)}, u32[]{:S(2)}) copy-start(bf16[1001,1152]{1,0:T(8,128)(2,1)} %param.17) | copy-start | bytes 6918916
  7.2 198.0 %all-gather.9.cloned.1.call-start = ((), (), s32[]{:S(2)}) async-start(), calls=%async_computation.8 | async-start | bytes 16920576 | tf_op jit(solution)/shard_map/all_gather | solution.py:194
  16.9 298.7 %all-gather.11.cloned.1.call-start = ((), (), s32[]{:S(2)}) async-start(), calls=%async_computation.9 | async-start | bytes 8460288 | tf_op jit(solution)/shard_map/all_gather | solution.py:190
  18.4 362.5 %all-gather.13.cloned.1.call-start = ((), (), s32[]{:S(2)}) async-start(), calls=%async_computation.10 | async-start | bytes 2820096 | tf_op jit(solution)/shard_map/all_gather | solution.py:191
  19.3 496.6 %all-gather.15.cloned.1.call-start = ((), (), s32[]{:S(2)}) async-start(), calls=%async_computation.11 | async-start | bytes 11280384 | tf_op jit(solution)/shard_map/all_gather | solution.py:192
  24.2 626.7 %all-gather.17.cloned.1.call-start = ((), (), s32[]{:S(2)}) async-start(), calls=%async_computation.12 | async-start | bytes 11280384 | tf_op jit(solution)/shard_map/all_gather | solution.py:193
  25.9 706.3 %all-gather.19.cloned.1.call-start = ((), (), s32[]{:S(2)}) async-start(), calls=%async_computation.13 | async-start | bytes 5013504 | tf_op jit(solution)/shard_map/all_gather | solution.py:195
  29.6 816.9 %all-gather.21.cloned.1.call-start = ((), (), s32[]{:S(2)}) async-start(), calls=%async_computation.14 | async-start | bytes 8912896 | tf_op jit(solution)/shard_map/all_gather | solution.py:196
  33.7 881.9 %all-gather.23.cloned.1.call-start = ((), (), s32[]{:S(2)}) async-start(), calls=%async_computation.15 | async-start | bytes 3342336 | tf_op jit(solution)/shard_map/all_gather | solution.py:197
  125.0 190.7 %copy-start.48 = (f32[4,128]{1,0:T(4,128)}, f32[4,128]{1,0:T(4,128)S(1)}, u32[]{:S(2)}) copy-start(f32[4,128]{1,0:T(4,128)S(1)} %broadcast_multiply_fusion.1) | copy-start | bytes 6148
  125.5 190.2 %copy-start.55 = (f32[4,128]{1,0:T(4,128)}, f32[4,128]{1,0:T(4,128)S(1)}, u32[]{:S(2)}) copy-start(f32[4,128]{1,0:T(4,128)S(1)} %fusion.94) | copy-start | bytes 6148
  213.0 111.5 %copy-start.41 = (f32[4,1152]{1,0:T(4,128)}, f32[4,1152]{1,0:T(4,128)S(1)}, u32[]{:S(2)}) copy-start(f32[4,1152]{1,0:T(4,128)S(1)} %get-tuple-element.51) | copy-start | bytes 55300
  213.0 303.0 %copy-start.59 = (f32[4,1152]{1,0:T(4,128)}, f32[4,1152]{1,0:T(4,128)S(1)}, u32[]{:S(2)}) copy-start(f32[4,1152]{1,0:T(4,128)S(1)} %get-tuple-element.48) | copy-start | bytes 55300
  327.1 17.0 collective-permute-start
  328.0 799.2 %reduce-scatter.11.cloned.1.call-start = ((), (), s32[]{:S(2)}) async-start(), calls=%async_computation.17 | async-start | bytes 3317760 | tf_op jit(solution)/shard_map/reduce_scatter | solution.py:315
  978.8 150.7 %reduce-scatter.23.cloned.1.call-start = ((), (), s32[]{:S(2)}) async-start(), calls=%async_computation.23 | async-start | bytes 3932160 | tf_op jit(solution)/shard_map/reduce_scatter | solution.py:333
  985.7 195.2 %reduce-scatter.19.cloned.1.call-start = ((), (), s32[]{:S(2)}) async-start(), calls=%async_computation.21 | async-start | bytes 5898240 | tf_op jit(solution)/shard_map/reduce_scatter | solution.py:327
  993.4 334.8 %reduce-scatter.21.cloned.1.call-start = ((), (), s32[]{:S(2)}) async-start(), calls=%async_computation.22 | async-start | bytes 10485760 | tf_op jit(solution)/shard_map/reduce_scatter | solution.py:330
  1004.4 465.6 %reduce-scatter.9.cloned.1.call-start = ((), (), s32[]{:S(2)}) async-start(), calls=%async_computation.16 | async-start | bytes 9953280 | tf_op jit(solution)/shard_map/reduce_scatter | solution.py:312
  1038.4 22.4 collective-permute-start.1
  1073.2 579.8 %reduce-scatter.13.cloned.1.call-start = ((), (), s32[]{:S(2)}) async-start(), calls=%async_computation.18 | async-start | bytes 13271040 | tf_op jit(solution)/shard_map/reduce_scatter | solution.py:318
  1085.0 751.4 %reduce-scatter.15.cloned.1.call-start = ((), (), s32[]{:S(2)}) async-start(), calls=%async_computation.19 | async-start | bytes 13271040 | tf_op jit(solution)/shard_map/reduce_scatter | solution.py:321
  1098.2 1009.1 %reduce-scatter.17.cloned.1.call-start = ((), (), s32[]{:S(2)}) async-start(), calls=%async_computation.20 | async-start | bytes 19906560 | tf_op jit(solution)/shard_map/reduce_scatter | solution.py:324
  1127.1 1208.1 %all-reduce.4.cloned.1.call-start = ((), (), s32[]{:S(2)}) async-start(), calls=%async_computation.24 | async-start | bytes 32014336 | tf_op jit(solution)/shard_map/psum | solution.py:342
  (85 other events, 1323.9 us)
Sparse Core Ops, SparseCore 0:
  17.1 188.0 all-gather.8
  208.5 107.1 all-gather.10
  318.4 62.4 all-gather.12
  383.5 132.4 all-gather.14
  519.2 131.6 all-gather.16
  653.5 78.6 all-gather.18
  735.0 111.4 all-gather.20
  849.2 66.3 all-gather.22
  978.9 51.1 reduce-scatter.10
  1032.8 59.9 reduce-scatter.22
  1095.6 85.2 reduce-scatter.18
  1183.1 144.9 reduce-scatter.20
  1331.1 138.7 reduce-scatter.8
  1472.3 180.6 reduce-scatter.12
  1655.2 181.1 reduce-scatter.14
  1838.8 268.4 reduce-scatter.16
  2124.0 211.2 all-reduce.3
where the time goes:
time: 2390 us; the launch traced here: 2380 us
  waiting for transfers between devices  1770 us (74%)
  matrix products  247 us (10%)
  local copies, waits for them, and re-layouts  137 us (6%)
  blocking collectives  133 us (6%)
  other arithmetic  73.7 us (3%)
    reduce_scatter x1, waiting for transfers between devices, body(): lax.psum_scatter(grad_wada.astype(jnp.bfloat16), 'inner', scatter_dimensi...  262 us
    reduce_scatter x1, waiting for transfers between devices, body(): lax.psum_scatter(grad_wup.astype(jnp.bfloat16), 'inner', scatter_dimensio...  175 us
    reduce_scatter x1, waiting for transfers between devices, body(): lax.psum_scatter(grad_wdown.astype(jnp.bfloat16), 'inner', scatter_dimens...  174 us
    psum x1, waiting for transfers between devices, body(): lax.psum(grid_w.astype(jnp.bfloat16), ('blk', 'outer')).astype(jnp.float32)  146 us
    reduce_scatter x1, waiting for transfers between devices, body(): lax.psum_scatter(grad_ptwo.astype(jnp.bfloat16), 'inner', scatter_dimensi...  144 us
    reduce_scatter x1, waiting for transfers between devices, body(): lax.psum_scatter(grad_wqkv.astype(jnp.bfloat16), 'inner', scatter_dimensi...  139 us
    all_gather x1, waiting for transfers between devices, body(): lax.all_gather(p_up, ('inner', 'outer'), axis=0, tiled=True)  128 us
    all_gather x1, waiting for transfers between devices, body(): lax.all_gather(p_down, ('inner', 'outer'), axis=0, tiled=True)  123 us
  transfers between devices with their start and end apart: 19, of which 15 were waited for; matrix products, arithmetic and copies ran while one was open for 13% of the time, Pallas kernels for 0%

commit v1 on v0

--- a/solution.py
+++ b/solution.py
@@ -339,7 +339,7 @@
     )
     grid_w, grid_b = outer_grid(inner_parts, n_outer)
     summed_w, summed_b = (
-        lax.psum(grid_w.astype(jnp.bfloat16), ("blk", "outer")).astype(jnp.float32),
+        lax.psum(lax.psum(grid_w.astype(jnp.bfloat16), "outer"), "blk").astype(jnp.float32),
         lax.psum(grid_b.astype(jnp.bfloat16), ("blk", "outer")).astype(jnp.float32),
     )
     own_index = lax.axis_index("outer")

time: 2390 us -> 2540 us (1.063)
  waiting for transfers between devices: 1770 us -> 1920 us
    psum x1 -> x2, waiting for transfers between devices: 146 us -> 295 us  [the longest x1 295 us: body(): lax.psum(grid_w.astype(jnp.bfloat16), 'outer')]
  transfers between devices with their start and end apart: 19 -> 20, of which waited for: 15 -> 15; matrix products, arithmetic and copies ran while one was open for 13% -> 13% of each run, Pallas kernels for 0% -> 0%
where the time goes in v1:
time: 2540 us; the launch traced here: 2530 us
  waiting for transfers between devices  1920 us (76%)
  matrix products  249 us (10%)
  local copies, waits for them, and re-layouts  137 us (5%)
  blocking collectives  131 us (5%)
  other arithmetic  73.7 us (3%)
    psum x1, waiting for transfers between devices, body(): lax.psum(grid_w.astype(jnp.bfloat16), 'outer')  295 us
    reduce_scatter x1, waiting for transfers between devices, body(): lax.psum_scatter(grad_wada.astype(jnp.bfloat16), 'inner', scatter_dimensi...  262 us
    reduce_scatter x1, waiting for transfers between devices, body(): lax.psum_scatter(grad_wup.astype(jnp.bfloat16), 'inner', scatter_dimensio...  175 us
    reduce_scatter x1, waiting for transfers between devices, body(): lax.psum_scatter(grad_wdown.astype(jnp.bfloat16), 'inner', scatter_dimens...  174 us
    reduce_scatter x1, waiting for transfers between devices, body(): lax.psum_scatter(grad_ptwo.astype(jnp.bfloat16), 'inner', scatter_dimensi...  144 us
    reduce_scatter x1, waiting for transfers between devices, body(): lax.psum_scatter(grad_wqkv.astype(jnp.bfloat16), 'inner', scatter_dimensi...  139 us
    all_gather x1, waiting for transfers between devices, body(): lax.all_gather(p_up, ('inner', 'outer'), axis=0, tiled=True)  128 us
    all_gather x1, waiting for transfers between devices, body(): lax.all_gather(p_down, ('inner', 'outer'), axis=0, tiled=True)  123 us
  transfers between devices with their start and end apart: 20, of which 15 were waited for; matrix products, arithmetic and copies ran while one was open for 13% of the time, Pallas kernels for 0%

profile of v1, /device:TPU:0, one launch (start us, length us, event | category | flops | bytes accessed | tf_op | source)
XLA Modules:
  0.0 2526.4 jit_solution(4056459929198751193)
XLA Ops:
  35.4 80.9 %all-reduce = bf16[20992]{0:T(1024)(128)(2,1)} all-reduce(bf16[20992]{0:T(1024)(128)(2,1)S(1)} %dynamic-update-slice), channel_id=1, replica_groups=mesh['blk'=2,'inner'=4,'outer'=4] {'inner','outer'}, use_global_device_ids=true, to_apply=%add | all-reduce | flops 20992 | bytes 83968
  125.7 79.5 %all-gather.9.cloned.1.call-done = bf16[1152,6912]{1,0:T(8,128)(2,1)} async-done(((bf16[72,6912]{1,0:T(8,128)(2,1)}), bf16[1152,6912]{1,0:T(8,128)(2,1)}) %all-gather.9.cloned.1.call-update) | async-done | bytes 15925264 | tf_op jit(solution)/shard_map/all_gather | solution.py:194
  213.0 102.7 %all-gather.11.cloned.1.call-done = bf16[1152,3456]{1,0:T(8,128)(2,1)} async-done(((bf16[72,3456]{1,0:T(8,128)(2,1)}), bf16[1152,3456]{1,0:T(8,128)(2,1)}) %all-gather.11.cloned.1.call-update) | async-done | bytes 7962640 | tf_op jit(solution)/shard_map/all_gather | solution.py:190
  365.8 15.1 all-gather.13.cloned.1.call-done
  388.3 127.6 %all-gather.15.cloned.1.call-done = bf16[1152,4608]{1,0:T(8,128)(2,1)} async-done(((bf16[72,4608]{1,0:T(8,128)(2,1)}), bf16[1152,4608]{1,0:T(8,128)(2,1)}) %all-gather.15.cloned.1.call-update) | async-done | bytes 10616848 | tf_op jit(solution)/shard_map/all_gather | solution.py:192
  528.1 122.7 %all-gather.17.cloned.1.call-done = bf16[4608,1152]{1,0:T(8,128)(2,1)} async-done(((bf16[288,1152]{1,0:T(8,128)(2,1)}), bf16[4608,1152]{1,0:T(8,128)(2,1)}) %all-gather.17.cloned.1.call-update) | async-done | bytes 10616848 | tf_op jit(solution)/shard_map/all_gather | solution.py:193
  650.9 14.5 add_convert_fusion.1
  665.4 66.8 %all-gather.19.cloned.1.call-done = bf16[1152,2048]{1,0:T(8,128)(2,1)} async-done(((bf16[72,2048]{1,0:T(8,128)(2,1)}), bf16[1152,2048]{1,0:T(8,128)(2,1)}) %all-gather.19.cloned.1.call-update) | async-done | bytes 4718608 | tf_op jit(solution)/shard_map/all_gather | solution.py:195
  738.9 107.6 %all-gather.21.cloned.1.call-done = bf16[2048,2048]{1,0:T(8,128)(2,1)} async-done(((bf16[128,2048]{1,0:T(8,128)(2,1)}), bf16[2048,2048]{1,0:T(8,128)(2,1)}) %all-gather.21.cloned.1.call-update) | async-done | bytes 8388624 | tf_op jit(solution)/shard_map/all_gather | solution.py:196
  857.7 57.9 %all-gather.23.cloned.1.call-done = bf16[2048,768]{1,0:T(8,128)(2,1)} async-done(((bf16[128,768]{1,0:T(8,128)(2,1)}), bf16[2048,768]{1,0:T(8,128)(2,1)}) %all-gather.23.cloned.1.call-update) | async-done | bytes 3145744 | tf_op jit(solution)/shard_map/all_gather | solution.py:197
  941.9 17.3 fusion.114
  959.2 12.2 multiply_reduce_fusion.7
  1085.1 13.1 fusion.1
  1132.1 48.8 %reduce-scatter.19.cloned.1.call-done = bf16[288,2048]{1,0:T(8,128)(2,1)} async-done(((bf16[1152,2048]{1,0:T(8,128)(2,1)}), bf16[288,2048]{1,0:T(8,128)(2,1)}) %reduce-scatter.19.cloned.1.call-update) | async-done | bytes 1179664 | tf_op jit(solution)/shard_map/reduce_scatter | solution.py:327
  1184.1 144.1 %reduce-scatter.21.cloned.1.call-done = bf16[512,2048]{1,0:T(8,128)(2,1)} async-done(((bf16[2048,2048]{1,0:T(8,128)(2,1)}), bf16[512,2048]{1,0:T(8,128)(2,1)}) %reduce-scatter.21.cloned.1.call-update) | async-done | bytes 2097168 | tf_op jit(solution)/shard_map/reduce_scatter | solution.py:330
  1331.4 138.6 %reduce-scatter.9.cloned.1.call-done = bf16[288,3456]{1,0:T(8,128)(2,1)} async-done(((bf16[1152,3456]{1,0:T(8,128)(2,1)}), bf16[288,3456]{1,0:T(8,128)(2,1)}) %reduce-scatter.9.cloned.1.call-update) | async-done | bytes 1990672 | tf_op jit(solution)/shard_map/reduce_scatter | solution.py:312
  1477.9 175.2 %reduce-scatter.13.cloned.1.call-done = bf16[288,4608]{1,0:T(8,128)(2,1)} async-done(((bf16[1152,4608]{1,0:T(8,128)(2,1)}), bf16[288,4608]{1,0:T(8,128)(2,1)}) %reduce-scatter.13.cloned.1.call-update) | async-done | bytes 2654224 | tf_op jit(solution)/shard_map/reduce_scatter | solution.py:318
  1662.9 173.6 %reduce-scatter.15.cloned.1.call-done = bf16[1152,1152]{1,0:T(8,128)(2,1)} async-done(((bf16[4608,1152]{1,0:T(8,128)(2,1)}), bf16[1152,1152]{1,0:T(8,128)(2,1)}) %reduce-scatter.15.cloned.1.call-update) | async-done | bytes 2654224 | tf_op jit(solution)/shard_map/reduce_scatter | solution.py:321
  1845.2 262.1 %reduce-scatter.17.cloned.1.call-done = bf16[288,6912]{1,0:T(8,128)(2,1)} async-done(((bf16[1152,6912]{1,0:T(8,128)(2,1)}), bf16[288,6912]{1,0:T(8,128)(2,1)}) %reduce-scatter.17.cloned.1.call-update) | async-done | bytes 3981328 | tf_op jit(solution)/shard_map/reduce_scatter | solution.py:324
  2123.9 295.5 %all-reduce.5.cloned.1.call-done = bf16[4,2000896]{1,0:T(4,128)(2,1)} async-done(((bf16[4,2000896]{1,0:T(4,128)(2,1)}), bf16[4,2000896]{1,0:T(4,128)(2,1)}) %all-reduce.5.cloned.1.call-update) | async-done | bytes 16007184 | tf_op jit(solution)/shard_map/psum | solution.py:342
  2424.6 19.4 all-reduce.1
  2444.2 26.8 %psum.31 = bf16[4,1312]{1,0:T(4,128)(2,1)S(1)} all-reduce(bf16[4,1312]{1,0:T(4,128)(2,1)S(1)} %convert_element_type.227), channel_id=1, replica_groups=mesh['blk'=2,'inner'=4,'outer'=4] {'blk','outer'}, use_global_device_ids=true, to_apply=%region_43.44 | all-reduce | flops 5248 | bytes 20992 | tf_op jit(solution)/shard_map/psum | solution.py:343
  2472.2 12.5 fusion.92
  2494.3 20.1 add_multiply_fusion
  (382 shorter events, 375.1 us)
Async XLA Ops:
  7.2 116.3 %copy-start = (bf16[1001,1152]{1,0:T(8,128)(2,1)S(1)}, bf16[1001,1152]{1,0:T(8,128)(2,1)}, u32[]{:S(2)}) copy-start(bf16[1001,1152]{1,0:T(8,128)(2,1)} %param.17) | copy-start | bytes 6918916
  7.2 198.0 %all-gather.9.cloned.1.call-start = ((), (), s32[]{:S(2)}) async-start(), calls=%async_computation.8 | async-start | bytes 16920576 | tf_op jit(solution)/shard_map/all_gather | solution.py:194
  16.9 298.7 %all-gather.11.cloned.1.call-start = ((), (), s32[]{:S(2)}) async-start(), calls=%async_computation.9 | async-start | bytes 8460288 | tf_op jit(solution)/shard_map/all_gather | solution.py:190
  18.4 362.5 %all-gather.13.cloned.1.call-start = ((), (), s32[]{:S(2)}) async-start(), calls=%async_computation.10 | async-start | bytes 2820096 | tf_op jit(solution)/shard_map/all_gather | solution.py:191
  19.3 496.6 %all-gather.15.cloned.1.call-start = ((), (), s32[]{:S(2)}) async-start(), calls=%async_computation.11 | async-start | bytes 11280384 | tf_op jit(solution)/shard_map/all_gather | solution.py:192
  24.2 626.7 %all-gather.17.cloned.1.call-start = ((), (), s32[]{:S(2)}) async-start(), calls=%async_computation.12 | async-start | bytes 11280384 | tf_op jit(solution)/shard_map/all_gather | solution.py:193
  25.9 706.3 %all-gather.19.cloned.1.call-start = ((), (), s32[]{:S(2)}) async-start(), calls=%async_computation.13 | async-start | bytes 5013504 | tf_op jit(solution)/shard_map/all_gather | solution.py:195
  29.6 816.9 %all-gather.21.cloned.1.call-start = ((), (), s32[]{:S(2)}) async-start(), calls=%async_computation.14 | async-start | bytes 8912896 | tf_op jit(solution)/shard_map/all_gather | solution.py:196
  33.7 881.9 %all-gather.23.cloned.1.call-start = ((), (), s32[]{:S(2)}) async-start(), calls=%async_computation.15 | async-start | bytes 3342336 | tf_op jit(solution)/shard_map/all_gather | solution.py:197
  125.0 190.7 %copy-start.48 = (f32[4,128]{1,0:T(4,128)}, f32[4,128]{1,0:T(4,128)S(1)}, u32[]{:S(2)}) copy-start(f32[4,128]{1,0:T(4,128)S(1)} %broadcast_multiply_fusion.1) | copy-start | bytes 6148
  125.5 190.2 %copy-start.55 = (f32[4,128]{1,0:T(4,128)}, f32[4,128]{1,0:T(4,128)S(1)}, u32[]{:S(2)}) copy-start(f32[4,128]{1,0:T(4,128)S(1)} %fusion.94) | copy-start | bytes 6148
  213.0 303.0 %copy-start.59 = (f32[4,1152]{1,0:T(4,128)}, f32[4,1152]{1,0:T(4,128)S(1)}, u32[]{:S(2)}) copy-start(f32[4,1152]{1,0:T(4,128)S(1)} %get-tuple-element.48) | copy-start | bytes 55300
  327.1 17.0 collective-permute-start
  328.0 799.2 %reduce-scatter.11.cloned.1.call-start = ((), (), s32[]{:S(2)}) async-start(), calls=%async_computation.17 | async-start | bytes 3317760 | tf_op jit(solution)/shard_map/reduce_scatter | solution.py:315
  978.8 150.7 %reduce-scatter.23.cloned.1.call-start = ((), (), s32[]{:S(2)}) async-start(), calls=%async_computation.23 | async-start | bytes 3932160 | tf_op jit(solution)/shard_map/reduce_scatter | solution.py:333
  985.7 195.2 %reduce-scatter.19.cloned.1.call-start = ((), (), s32[]{:S(2)}) async-start(), calls=%async_computation.21 | async-start | bytes 5898240 | tf_op jit(solution)/shard_map/reduce_scatter | solution.py:327
  993.4 334.8 %reduce-scatter.21.cloned.1.call-start = ((), (), s32[]{:S(2)}) async-start(), calls=%async_computation.22 | async-start | bytes 10485760 | tf_op jit(solution)/shard_map/reduce_scatter | solution.py:330
  1004.4 465.6 %reduce-scatter.9.cloned.1.call-start = ((), (), s32[]{:S(2)}) async-start(), calls=%async_computation.16 | async-start | bytes 9953280 | tf_op jit(solution)/shard_map/reduce_scatter | solution.py:312
  1038.4 22.4 collective-permute-start.1
  1073.2 579.8 %reduce-scatter.13.cloned.1.call-start = ((), (), s32[]{:S(2)}) async-start(), calls=%async_computation.18 | async-start | bytes 13271040 | tf_op jit(solution)/shard_map/reduce_scatter | solution.py:318
  1085.0 751.4 %reduce-scatter.15.cloned.1.call-start = ((), (), s32[]{:S(2)}) async-start(), calls=%async_computation.19 | async-start | bytes 13271040 | tf_op jit(solution)/shard_map/reduce_scatter | solution.py:321
  1098.2 1009.1 %reduce-scatter.17.cloned.1.call-start = ((), (), s32[]{:S(2)}) async-start(), calls=%async_computation.20 | async-start | bytes 19906560 | tf_op jit(solution)/shard_map/reduce_scatter | solution.py:324
  1127.1 1292.3 %all-reduce.5.cloned.1.call-start = ((), (), s32[]{:S(2)}) async-start(), calls=%async_computation.24 | async-start | bytes 32014336 | tf_op jit(solution)/shard_map/psum | solution.py:342
  2123.8 360.9 %all-reduce.7.cloned.1.call-start = ((), (), s32[]{:S(2)}) async-start(), calls=%async_computation.25 | async-start | bytes 32014336 | tf_op jit(solution)/shard_map/psum | solution.py:342
  (86 other events, 1432.6 us)
Sparse Core Ops, SparseCore 0:
  17.1 188.0 all-gather.8
  208.5 107.1 all-gather.10
  318.4 62.4 all-gather.12
  383.5 132.4 all-gather.14
  519.2 131.6 all-gather.16
  653.5 78.6 all-gather.18
  735.0 111.4 all-gather.20
  849.2 66.3 all-gather.22
  978.9 51.1 reduce-scatter.10
  1032.8 59.9 reduce-scatter.22
  1095.6 85.2 reduce-scatter.18
  1183.1 144.9 reduce-scatter.20
  1331.1 138.7 reduce-scatter.8
  1472.3 180.6 reduce-scatter.12
  1655.2 181.1 reduce-scatter.14
  1838.8 268.4 reduce-scatter.16
  2123.9 295.3 all-reduce.4
  2421.8 59.2 all-reduce.6
